TPU v7x, 32 devices: a whole 2x2x4 slice. The times are simulated.
32 devices in a mesh: dp: 4 (over z), ctx: 4 (over y, core), tensor: 2 (over x).
Axes of the slice: x: 2, y: 2, z: 4, core: 2. Of those that a mesh axis runs over, the one named last changes fastest.
Arguments:
- tokens: bfloat16 [4096, 1536], P(('dp', 'ctx'), 'tensor'), may hold values from -6 to 6
- segments: int32 [4, 1024], P('dp'), may hold values from 0 to 1, never falling along the last dimension, each value on 1 to 768 neighbouring positions
- order: int32 [4, 1024], P('dp'), may hold values from 0 to 1023, each once within a row
- routes: int32 [4096, 8], P('dp'), may hold values from 0 to 39, all different within a row
- gain_one: float32 [1536], P('tensor'), may hold values from 0.5 to 1.5
- w_query: bfloat16 [1536, 1536], P('dp', 'tensor'), may hold values from -0.15625 to 0.15625
- w_key: bfloat16 [1536, 512], P('dp', 'tensor'), may hold values from -0.15625 to 0.15625
- w_value: bfloat16 [1536, 512], P('dp', 'tensor'), may hold values from -0.15625 to 0.15625
- w_output: bfloat16 [1536, 1536], P('dp', 'tensor'), may hold values from -1.25 to 1.25
- gain_two: float32 [1536], P('tensor'), may hold values from 0.5 to 1.5
- w_router: bfloat16 [1536, 40], P('dp'), may hold values from -0.06982422 to 0.06982422
- w_expert_in: bfloat16 [1536, 40, 1024], P('dp', 'tensor'), may hold values from -0.15625 to 0.15625
- w_expert_out: bfloat16 [1536, 40, 512], P('dp', 'tensor'), may hold values from -0.75 to 0.75
- cotangent: bfloat16 [4096, 1536], P(('dp', 'ctx'), 'tensor'), may hold values from -6 to 6
Outputs:
- output: bfloat16 [4096, 1536], P(('dp', 'ctx'), 'tensor')
- grad_tokens: float32 [4096, 1536], P(('dp', 'ctx'), 'tensor')
- grad_gain_one: float32 [1536], P('tensor')
- grad_query: float32 [1536, 1536], P('dp', 'tensor')
- grad_key: float32 [1536, 512], P('dp', 'tensor')
- grad_value: float32 [1536, 512], P('dp', 'tensor')
- grad_output: float32 [1536, 1536], P('dp', 'tensor')
- grad_gain_two: float32 [1536], P('tensor')
- grad_router: float32 [1536, 40], P('dp')
- grad_expert_in: float32 [1536, 40, 1024], P('dp', 'tensor')
- grad_expert_out: float32 [1536, 40, 512], P('dp', 'tensor')
Inputs may be any that keep to these rules, and one draw needn't show every extreme that they name: `routes`: each row names 8 different experts. `segments`: in each pack the document numbers never fall and each of the 2 documents has at least one token; no document has more than 768 tokens. `order`: each row names every position of its pack once.
All inputs are finite; a program needn't handle non-finite values.
Results may differ from a plain program's by a relative error of at most 0.015.
Values may be sent and summed in bfloat16 or wider, within the bound.
A program may use at most 640 MiB of HBM per device.

v0:
```python
import jax
import jax.numpy as jnp
from jax import lax
from jax.sharding import PartitionSpec as P

D = 1536
HEAD_DIM = 64
EXPERTS = 40
TOP_K = 8
FF = 512
EPS = 1e-06
THETA = 10000.0
NEG = -1e30
LANES = 128
ALL = ("dp", "ctx", "tensor")
BF = jnp.bfloat16
F32 = jnp.float32


def rope_tables(position):
    halves = HEAD_DIM // 2
    frequency = THETA ** (-2.0 * jnp.arange(halves, dtype=F32) / HEAD_DIM)
    angles = position[:, None] * frequency[None, :]
    return (jnp.cos(angles)[:, None, :], jnp.sin(angles)[:, None, :])


def rotate(values, cosine_table, sine_table):
    halves = values.shape[-1] // 2
    first_half, second_half = (values[..., :halves], values[..., halves:])
    return jnp.concatenate(
        [
            first_half * cosine_table - second_half * sine_table,
            second_half * cosine_table + first_half * sine_table,
        ],
        axis=-1,
    )


def dot(a, b, dims):
    return lax.dot_general(a, b, (dims, ((), ())), preferred_element_type=F32)


def norm_forward(rows, gain):
    inverse = lax.rsqrt(jnp.mean(rows * rows, axis=1, keepdims=True) + EPS)
    return (inverse, (rows * inverse * gain[None, :]).astype(BF))


def norm_backward(rows, gain, inverse, grad_normed):
    weighted = grad_normed * gain[None, :]
    inner = jnp.sum(weighted * rows, axis=1, keepdims=True)
    grad_rows = weighted * inverse - rows * (inverse * inverse * inverse * inner / D)
    return (grad_rows, jnp.sum(grad_normed * rows * inverse, axis=0))


def exchange(parts, at, count):
    result = lax.dynamic_update_index_in_dim(
        jnp.zeros_like(parts), lax.dynamic_index_in_dim(parts, at, 0), at, 0
    )
    for hop in range(1, count):
        sent = lax.dynamic_index_in_dim(parts, (at + hop) % count, 0)
        got = lax.ppermute(sent, "dp", [(i, (i + hop) % count) for i in range(count)])
        result = lax.dynamic_update_index_in_dim(result, got, (at - hop) % count, 0)
    return result


def on_device(
    tokens,
    segments,
    order,
    routes,
    gain_one,
    w_query,
    w_key,
    w_value,
    w_output,
    gain_two,
    w_router,
    w_expert_in,
    w_expert_out,
    cotangent,
):
    nd, nc, nt = (lax.axis_size("dp"), lax.axis_size("ctx"), lax.axis_size("tensor"))
    dp_at, ctx_at, tensor_at = (
        lax.axis_index("dp"),
        lax.axis_index("ctx"),
        lax.axis_index("tensor"),
    )
    n_rows, part_width = tokens.shape
    sub = n_rows // nt
    pack_len = order.shape[1]
    d_local = w_query.shape[0]
    q_width, kv_width = (w_query.shape[1], w_key.shape[1])
    q_heads, kv_heads = (q_width // HEAD_DIM, kv_width // HEAD_DIM)
    group = q_heads // kv_heads
    qkv_width = q_width + 2 * kv_width
    local_count = w_expert_in.shape[1]
    capacity = n_rows * 3 // 8
    gains = lax.all_gather(jnp.stack([gain_one, gain_two]), "tensor", axis=1, tiled=True)
    gain_one_full, gain_two_full = (gains[0], gains[1])
    tokens_full = lax.all_gather(tokens, "tensor", axis=1, tiled=True)
    packed = jnp.concatenate([w_query, w_key, w_value, w_router], axis=1)
    share = d_local // nc
    packed = lax.dynamic_slice_in_dim(packed, ctx_at * share, share, 0)
    packed = lax.all_gather(packed, ("dp", "ctx"), axis=0, tiled=True)
    qkv_w, router_w = (packed[:, :qkv_width], packed[:, qkv_width:])
    output_w = lax.all_gather(
        lax.dynamic_slice_in_dim(w_output, ctx_at * share, share, 0),
        ("dp", "ctx"),
        axis=0,
        tiled=True,
    )
    cot_sub = lax.all_to_all(cotangent, "tensor", 0, 1, tiled=True)
    cot_all = lax.all_gather(cot_sub, ALL, axis=0, tiled=True)
    tokens_sub = lax.dynamic_slice_in_dim(tokens_full, tensor_at * sub, sub, 0).astype(F32)
    by_expert = local_count % nc == 0
    own_count = local_count // nc if by_expert else local_count
    units = FF // nd if by_expert else FF // (nd * nc)
    first_expert = tensor_at * local_count + (ctx_at * own_count if by_expert else 0)
    if by_expert:
        own_in = lax.dynamic_slice_in_dim(w_expert_in, ctx_at * own_count, own_count, 1)
        own_out = lax.dynamic_slice_in_dim(w_expert_out, ctx_at * own_count, own_count, 1)
        own_in = own_in.reshape(d_local, own_count, 2, nd, units)
        own_out = own_out.reshape(d_local, own_count, nd, units)
    else:
        own_in = w_expert_in.reshape(d_local, own_count, 2, nd, nc, units)
        own_out = w_expert_out.reshape(d_local, own_count, nd, nc, units)
        own_in = lax.dynamic_index_in_dim(own_in, ctx_at, 4, False)
        own_out = lax.dynamic_index_in_dim(own_out, ctx_at, 3, False)
    own_in = jnp.transpose(own_in, (3, 0, 2, 1, 4)).reshape(nd, d_local, 2 * own_count * units)
    own_out = jnp.transpose(own_out, (2, 0, 1, 3)).reshape(nd, d_local, own_count * units)
    width = own_count * units
    expert_w = exchange(jnp.concatenate([own_in, own_out], axis=2), dp_at, nd)
    expert_w = expert_w.reshape(D, 3 * width)
    upper_w, lower_w = (expert_w[:, : 2 * width], expert_w[:, 2 * width :])
    order_row = order[0]
    places = jnp.arange(pack_len, dtype=jnp.int32)
    dealt = jnp.sum(jnp.where(order_row[:, None] == places[None, :], places[:, None], 0), axis=0)
    sub_start = ctx_at * n_rows + tensor_at * sub
    dealt_sub = lax.dynamic_slice_in_dim(dealt, sub_start, sub)
    experts_all = jnp.arange(EXPERTS, dtype=jnp.int32)
    uses = jnp.any(routes[:, :, None] == experts_all[None, None, :], axis=1)
    earlier = (dealt_sub[:, None] // n_rows == dealt[None, :] // n_rows) & (
        dealt[None, :] < dealt_sub[:, None]
    )
    ranks = dot(earlier.astype(BF), uses.astype(BF), ((1,), (0,)))
    uses_sub = lax.dynamic_slice_in_dim(uses, sub_start, sub, 0)
    kept = (uses_sub & (ranks < capacity)).astype(F32)
    segment_row = segments[0]
    local_segs = lax.dynamic_slice_in_dim(segment_row, ctx_at * n_rows, n_rows)
    local_places = ctx_at * n_rows + jnp.arange(n_rows, dtype=jnp.int32)
    starts = jnp.sum((segment_row[None, :] < local_segs[:, None]).astype(jnp.int32), axis=1)
    cosine_table, sine_table = rope_tables((local_places - starts).astype(F32))
    _, h_one = norm_forward(tokens_full.astype(F32), gain_one_full)
    projected = dot(h_one, qkv_w, ((1,), (0,)))
    turned = rotate(
        projected[:, : q_width + kv_width].reshape(n_rows, q_heads + kv_heads, HEAD_DIM),
        cosine_table,
        sine_table,
    ).astype(BF)
    queries = turned[:, :q_heads].reshape(n_rows, kv_heads, group, HEAD_DIM)
    kv_rows = jnp.concatenate(
        [
            turned[:, q_heads:].reshape(n_rows, kv_width),
            projected[:, q_width + kv_width :].astype(BF),
        ],
        axis=1,
    )
    kv_all = lax.all_gather(kv_rows, "ctx", axis=0, tiled=True)
    key_heads = kv_all[:, :kv_width].reshape(pack_len, kv_heads, HEAD_DIM)
    value_heads = kv_all[:, kv_width:].reshape(pack_len, kv_heads, HEAD_DIM)
    allowed = (local_segs[:, None] == segment_row[None, :]) & (
        local_places[:, None] >= places[None, :]
    )
    score_scale = HEAD_DIM ** (-0.5)
    scores = score_scale * jnp.einsum(
        "bagd,pad->agbp", queries, key_heads, preferred_element_type=F32
    )
    scores = jnp.where(allowed[None, None], scores, NEG)
    highest = jnp.max(scores, axis=-1, keepdims=True)
    weights = jnp.exp(scores - highest)
    totals = jnp.sum(weights, axis=-1, keepdims=True)
    shares_low = (weights / totals).astype(BF)
    log_totals = highest + jnp.log(totals)
    attended = (
        jnp.einsum("agbp,pad->bagd", shares_low, value_heads, preferred_element_type=F32)
        .astype(BF)
        .reshape(n_rows, q_width)
    )
    attended_sub = lax.all_to_all(attended, "tensor", 0, 1, tiled=True)
    output_full = lax.all_gather(output_w, "tensor", axis=1, tiled=True)
    middle = tokens_sub + dot(attended_sub, output_full, ((1,), (1,)))
    inverse_two, h_two = norm_forward(middle, gain_two_full)
    logits = jnp.where(uses_sub, dot(h_two, router_w, ((1,), (0,))), NEG)
    raised = jnp.exp(logits - jnp.max(logits, axis=1, keepdims=True))
    gates = raised / jnp.sum(raised, axis=1, keepdims=True)
    gates_kept = gates * kept
    gates_high = gates_kept.astype(BF)
    gates_low = (gates_kept - gates_high.astype(F32)).astype(BF)
    extra = jnp.zeros((sub, LANES - 2 * EXPERTS), BF)
    h_all = lax.all_gather(
        jnp.concatenate([h_two, gates_high, gates_low, extra], axis=1), ALL, axis=0, tiled=True
    )
    gates_all = h_all[:, D : D + EXPERTS].astype(F32) + h_all[
        :, D + EXPERTS : D + 2 * EXPERTS
    ].astype(F32)
    total_rows = h_all.shape[0]
    gates_own = lax.dynamic_slice_in_dim(gates_all, first_expert, own_count, 1)
    h_all = h_all[:, :D]
    gate_wide = jnp.broadcast_to(gates_own[:, :, None], (total_rows, own_count, units)).reshape(
        total_rows, width
    )
    hidden = dot(h_all, upper_w, ((1,), (0,)))
    grad_raw = dot(cot_all, lower_w, ((1,), (0,)))
    gate_part, up_part = (hidden[:, :width], hidden[:, width:])
    sigmoid = jax.nn.sigmoid(gate_part)
    silu = gate_part * sigmoid
    active = (silu * up_part).astype(BF).astype(F32)
    active_gated = (active * gate_wide).astype(BF)
    grad_gates = jnp.sum((grad_raw * active).reshape(total_rows, own_count, units), axis=2)
    grad_active = grad_raw * gate_wide
    grad_hidden = jnp.concatenate(
        [grad_active * up_part * sigmoid * (1.0 + gate_part * (1.0 - sigmoid)), grad_active * silu],
        axis=1,
    ).astype(BF)
    grad_in = dot(grad_hidden, upper_w, ((1,), (1,))).astype(BF)
    grad_gates = lax.dynamic_update_slice_in_dim(
        jnp.zeros((total_rows, LANES), BF), grad_gates.astype(BF), first_expert, 1
    )
    mixed = dot(active_gated, lower_w, ((1,), (1,))).astype(BF)
    back_sub = lax.psum_scatter(
        jnp.concatenate([grad_in, grad_gates], axis=1), ALL, scatter_dimension=0, tiled=True
    ).astype(F32)
    mixed_sub = lax.psum_scatter(mixed, ALL, scatter_dimension=0, tiled=True).astype(F32)
    grad_upper = dot(h_all, grad_hidden, ((0,), (0,))).astype(BF)
    grad_lower = dot(cot_all, active_gated, ((0,), (0,))).astype(BF)
    grad_expert = jnp.concatenate([grad_upper, grad_lower], axis=1).reshape(nd, d_local, 3 * width)
    grad_expert = exchange(grad_expert, dp_at, nd)
    grad_expert = lax.all_gather(grad_expert, "ctx", axis=0)
    grad_up = grad_expert[..., : 2 * width].reshape(nc, nd, d_local, 2, own_count, units)
    grad_low = grad_expert[..., 2 * width :].reshape(nc, nd, d_local, own_count, units)
    if by_expert:
        grad_up = jnp.transpose(grad_up, (2, 0, 4, 3, 1, 5))
        grad_low = jnp.transpose(grad_low, (2, 0, 3, 1, 4))
    else:
        grad_up = jnp.transpose(grad_up, (2, 4, 3, 1, 0, 5))
        grad_low = jnp.transpose(grad_low, (2, 3, 1, 0, 4))
    grad_expert_in = grad_up.reshape(d_local, local_count, 2 * FF).astype(F32)
    grad_expert_out = grad_low.reshape(d_local, local_count, FF).astype(F32)
    result = lax.all_to_all((middle + mixed_sub).astype(BF), "tensor", 1, 0, tiled=True)
    gate_grads = back_sub[:, D : D + EXPERTS] * kept
    logit_grads = (
        gates * (gate_grads - jnp.sum(gates * gate_grads, axis=1, keepdims=True))
    ).astype(BF)
    grad_norm_two = back_sub[:, :D] + dot(logit_grads, router_w, ((1,), (1,)))
    grad_middle, grad_gain_two = norm_backward(middle, gain_two_full, inverse_two, grad_norm_two)
    grad_middle = grad_middle + cot_sub.astype(F32)
    extra = jnp.zeros((sub, LANES - EXPERTS), BF)
    grad_attn = lax.all_gather(
        jnp.concatenate([grad_middle.astype(BF), logit_grads, extra], axis=1),
        "tensor",
        axis=0,
        tiled=True,
    )
    logit_grads_full = grad_attn[:, D : D + EXPERTS]
    grad_attn = grad_attn[:, :D]
    h_two_full = lax.dynamic_slice_in_dim(h_all, (dp_at * nc + ctx_at) * n_rows, n_rows, 0)
    grad_router = dot(h_two_full, logit_grads_full, ((0,), (0,)))
    grad_output_w = dot(grad_attn, attended, ((0,), (0,)))
    grad_blended = (
        dot(grad_attn, output_w, ((1,), (0,))).astype(BF).reshape(n_rows, kv_heads, group, HEAD_DIM)
    )
    shares = jnp.exp(scores - log_totals)
    grad_shares = jnp.einsum(
        "bagd,pad->agbp", grad_blended, value_heads, preferred_element_type=F32
    )
    inner = jnp.sum(shares * grad_shares, axis=-1, keepdims=True)
    grad_scores = (shares * (grad_shares - inner)).astype(BF)
    grad_queries = score_scale * jnp.einsum(
        "agbp,pad->bagd", grad_scores, key_heads, preferred_element_type=F32
    )
    grad_keys = score_scale * jnp.einsum(
        "agbp,bagd->pad", grad_scores, queries, preferred_element_type=F32
    )
    grad_values = jnp.einsum("agbp,bagd->pad", shares_low, grad_blended, preferred_element_type=F32)
    grad_kv = lax.psum_scatter(
        jnp.concatenate(
            [grad_keys.reshape(pack_len, kv_width), grad_values.reshape(pack_len, kv_width)], axis=1
        ).astype(BF),
        "ctx",
        scatter_dimension=0,
        tiled=True,
    ).astype(F32)
    grad_turned = jnp.concatenate(
        [
            grad_queries.reshape(n_rows, q_heads, HEAD_DIM),
            grad_kv[:, :kv_width].reshape(n_rows, kv_heads, HEAD_DIM),
        ],
        axis=1,
    )
    grad_qkv = jnp.concatenate(
        [
            rotate(grad_turned, cosine_table, -sine_table)
            .astype(BF)
            .reshape(n_rows, q_width + kv_width),
            grad_kv[:, kv_width:].astype(BF),
        ],
        axis=1,
    )
    qkv_full = lax.all_gather(qkv_w, "tensor", axis=1, tiled=True)
    grad_qkv_sub = lax.all_to_all(grad_qkv, "tensor", 0, 1, tiled=True)
    grad_norm_one = dot(grad_qkv_sub, qkv_full, ((1,), (1,)))
    inverse_sub = lax.rsqrt(jnp.mean(tokens_sub * tokens_sub, axis=1, keepdims=True) + EPS)
    grad_tokens, grad_gain_one = norm_backward(
        tokens_sub, gain_one_full, inverse_sub, grad_norm_one
    )
    grad_tokens = lax.all_to_all(grad_tokens + grad_middle, "tensor", 1, 0, tiled=True)
    grad_qkv_w = dot(h_one, grad_qkv, ((0,), (0,)))
    weight_grads = jnp.concatenate([grad_qkv_w, grad_output_w, grad_router], axis=1).astype(BF)
    weight_grads = lax.psum_scatter(weight_grads, ("dp", "ctx"), scatter_dimension=0, tiled=True)
    weight_grads = lax.all_gather(weight_grads, "ctx", axis=0, tiled=True).astype(F32)
    edges = [0, q_width, q_width + kv_width, qkv_width, qkv_width + q_width]
    gain_grads = lax.psum(jnp.stack([grad_gain_one, grad_gain_two]), ALL)
    gain_grads = lax.dynamic_slice_in_dim(gain_grads, tensor_at * part_width, part_width, 1)
    return (
        result,
        grad_tokens,
        gain_grads[0],
        weight_grads[:, edges[0] : edges[1]],
        weight_grads[:, edges[1] : edges[2]],
        weight_grads[:, edges[2] : edges[3]],
        weight_grads[:, edges[3] : edges[4]],
        gain_grads[1],
        weight_grads[:, edges[4] :],
        grad_expert_in,
        grad_expert_out,
    )


def solution(mesh):
    return jax.shard_map(
        on_device,
        mesh=mesh,
        in_specs=(
            P(("dp", "ctx"), "tensor"),
            P("dp", None),
            P("dp", None),
            P("dp", None),
            P("tensor"),
            P("dp", "tensor"),
            P("dp", "tensor"),
            P("dp", "tensor"),
            P("dp", "tensor"),
            P("tensor"),
            P("dp", None),
            P("dp", "tensor", None),
            P("dp", "tensor", None),
            P(("dp", "ctx"), "tensor"),
        ),
        out_specs=(
            P(("dp", "ctx"), "tensor"),
            P(("dp", "ctx"), "tensor"),
            P("tensor"),
            P("dp", "tensor"),
            P("dp", "tensor"),
            P("dp", "tensor"),
            P("dp", "tensor"),
            P("tensor"),
            P("dp", None),
            P("dp", "tensor", None),
            P("dp", "tensor", None),
        ),
        check_vma=False,
    )
```

profile of v0, /device:TPU:0, one launch (start us, length us, event | category | flops | bytes accessed | tf_op | source)
XLA Modules:
  0.0 1732.6 jit_solution(15310656353392868599)
XLA Ops:
  13.2 5.3 all_gather.48
  20.2 10.7 all_gather.47
  31.9 32.8 %all-gather.10.cloned.1.call-done = bf16[1536,1320]{1,0:T(8,128)(2,1)} async-done(((bf16[96,1320]{1,0:T(8,128)(2,1)}), bf16[1536,1320]{1,0:T(8,128)(2,1)}) %all-gather.10.cloned.1.call-update) | async-done | bytes 4055056 | tf_op jit(solution)/shard_map/all_gather | solution.py:104
  64.7 3.4 fusion.51
  70.5 37.9 %all-gather.14.cloned.1.call-done = bf16[1536,768]{1,0:T(8,128)(2,1)} async-done(((bf16[96,768]{1,0:T(8,128)(2,1)}), bf16[1536,768]{1,0:T(8,128)(2,1)}) %all-gather.14.cloned.1.call-update) | async-done | bytes 2359312 | tf_op jit(solution)/shard_map/all_gather | solution.py:106
  108.9 17.1 all-gather.12.cloned.1.call-done
  134.1 3.2 copy-done.2
  144.9 3.6 all-to-all-start
  149.1 45.2 %all-gather.16.cloned.1.call-done = bf16[1536,1536]{1,0:T(8,128)(2,1)} async-done(((bf16[1536,768]{1,0:T(8,128)(2,1)}), bf16[1536,1536]{1,0:T(8,128)(2,1)}) %all-gather.16.cloned.1.call-update) | async-done | bytes 4718608 | tf_op jit(solution)/shard_map/all_gather | solution.py:190
  194.3 3.7 multiply_reduce_fusion.2
  201.1 9.1 all_to_all.92
  211.2 4.7 constant_dynamic-slice_fusion.4
  215.9 6.3 copy.311
  222.2 4.7 copy.262
  230.0 4.0 copy.312
  234.0 3.1 copy.264
  237.1 5.4 fusion.17
  254.7 37.0 %collective-permute-done = bf16[1,384,1920]{1,2,0:T(8,128)(2,1)} collective-permute-done((bf16[1,384,1920]{1,2,0:T(8,128)(2,1)}, bf16[1,384,1920]{1,2,0:T(8,128)(2,1)}, u32[]{:S(2)}, u32[]{:S(2)}) %collective-permute-start) | collective-permute-done | bytes 1474592 | tf_op jit(solution)/shard_map/ppermute | solution.py:61
  294.3 77.8 %collective-permute-done.1 = bf16[1,384,1920]{1,2,0:T(8,128)(2,1)} collective-permute-done((bf16[1,384,1920]{1,2,0:T(8,128)(2,1)}, bf16[1,384,1920]{1,2,0:T(8,128)(2,1)}, u32[]{:S(2)}, u32[]{:S(2)}) %collective-permute-start.1) | collective-permute-done | bytes 1474592 | tf_op jit(solution)/shard_map/ppermute | solution.py:61
  383.8 50.0 %all-gather.18.cloned.1.call-done = bf16[4096,1664]{0,1:T(8,128)(2,1)} async-done(((bf16[128,1664]{0,1:T(8,128)(2,1)}), bf16[4096,1664]{0,1:T(8,128)(2,1)}) %all-gather.18.cloned.1.call-update) | async-done | bytes 13631504 | tf_op jit(solution)/shard_map/all_gather | solution.py:200
  434.9 22.6 %fusion.8 = f32[4096,1280]{0,1:T(8,128)} fusion(bf16[1536,1920]{1,0:T(8,128)(2,1)} %bitcast.22, bf16[4096,1664]{0,1:T(8,128)(2,1)} %all-gather.18.cloned.1.call-done), kind=kOutput, calls=%fused_computation.41 | convolution fusion | flops 16106127360 | bytes 37486592 | tf_op jit(solution)/shard_map/dot_general | solution.py:40
  457.6 103.0 %all-gather.20.cloned.1.call-done = bf16[4096,1536]{0,1:T(8,128)(2,1)} async-done(((bf16[128,1536]{0,1:T(8,128)(2,1)}), bf16[4096,1536]{0,1:T(8,128)(2,1)}) %all-gather.20.cloned.1.call-update) | async-done | bytes 12582928 | tf_op jit(solution)/shard_map/all_gather | solution.py:113
  560.6 28.3 %multiply_convert_fusion.1 = (bf16[4096,640]{0,1:T(8,128)(2,1)}, bf16[4096,640]{0,1:T(8,128)(2,1)}, f32[4096,640]{0,1:T(8,128)}, bf16[4096,640]{0,1:T(8,128)(2,1)}) fusion(f32[4096,1280]{0,1:T(8,128)} %fusion.8, f32[4096,5]{0,1:T(8,128)S(1)} %convert_add_fusion.1, bf16[4096,1536]{0,1:T(8,128)(2,1)} %all-gather.20.cloned.1.call-done, ...), kind=kOutput, calls=%fused_computation.21 | convolution fusion | flops 8100249600 | bytes 61816832 | tf_op jit(solution)/shard_map/dot_general | solution.py:40
  588.9 4.7 reduce_sum.132
  593.6 23.4 %convolution_convert_fusion.1 = bf16[4096,1536]{0,1:T(8,128)(2,1)} fusion(bf16[4096,640]{0,1:T(8,128)(2,1)} %get-tuple-element.101, bf16[4096,640]{0,1:T(8,128)(2,1)} %get-tuple-element.100, bf16[1536,1920]{1,0:T(8,128)(2,1)} %bitcast.22), kind=kOutput, calls=%fused_computation.5 | convolution fusion | flops 16133390336 | bytes 27000832 | tf_op jit(solution)/shard_map/dot_general | solution.py:40
  619.7 14.8 pad_maximum_fusion
  634.4 17.9 %copy.306 = bf16[4096,1664]{1,0:T(8,128)(2,1)} copy(bf16[4096,1664]{0,1:T(8,128)(2,1)} %pad_maximum_fusion) | data formatting | bytes 27262976
  652.5 290.2 %reduce-scatter.15.cloned.1.call-done = bf16[128,1664]{1,0:T(8,128)(2,1)} async-done(((bf16[4096,1664]{1,0:T(8,128)(2,1)}), bf16[128,1664]{1,0:T(8,128)(2,1)}) %reduce-scatter.15.cloned.1.call-update) | async-done | bytes 426000
  947.6 13.2 all_gather.55
  963.4 5.7 fusion.24
  969.1 6.9 fusion
  976.3 4.8 fusion.2
  981.1 4.8 fusion.23
  987.1 3.8 fusion.4
  993.3 14.0 convolution_convert_fusion
  1007.4 4.3 slice.148
  1011.8 13.1 fusion.10
  1024.9 23.4 %convolution_convert_fusion.2 = bf16[1536,1280]{0,1:T(8,128)(2,1)S(1)} fusion(bf16[4096,640]{0,1:T(8,128)(2,1)} %get-tuple-element.101, bf16[4096,640]{0,1:T(8,128)(2,1)} %get-tuple-element.100, bf16[4096,1664]{0,1:T(8,128)(2,1)} %all-gather.18.cloned.1.call-done), kind=kOutput, calls=%fused_computation.29 | convolution fusion | flops 16129064960 | bytes 27000832 | tf_op jit(solution)/shard_map/dot_general | solution.py:40
  1051.3 8.8 copy.310
  1073.4 49.4 %collective-permute-done.3 = bf16[1,384,1920]{2,1,0:T(8,128)(2,1)S(1)} collective-permute-done((bf16[1,384,1920]{2,1,0:T(8,128)(2,1)S(1)}, bf16[1,384,1920]{2,1,0:T(8,128)(2,1)S(1)}, u32[]{:S(2)}, u32[]{:S(2)}) %collective-permute-start.3) | collective-permute-done | bytes 1474592 | tf_op jit(solution)/shard_map/ppermute | solution.py:61
  1124.1 72.0 %collective-permute-done.4 = bf16[1,384,1920]{2,1,0:T(8,128)(2,1)S(1)} collective-permute-done((bf16[1,384,1920]{2,1,0:T(8,128)(2,1)S(1)}, bf16[1,384,1920]{2,1,0:T(8,128)(2,1)S(1)}, u32[]{:S(2)}, u32[]{:S(2)}) %collective-permute-start.4) | collective-permute-done | bytes 1474592 | tf_op jit(solution)/shard_map/ppermute | solution.py:61
  1199.1 5.5 slice-done.5
  1218.1 9.2 copy.308
  1227.5 4.2 pad_maximum_fusion.7
  1232.7 3.5 all-to-all-start.3
  1236.4 27.6 %reduce-scatter.13.cloned.1.call-done = bf16[128,1536]{1,0:T(8,128)(2,1)} async-done(((bf16[4096,1536]{1,0:T(8,128)(2,1)}), bf16[128,1536]{1,0:T(8,128)(2,1)}) %reduce-scatter.13.cloned.1.call-update) | async-done | bytes 393232
  1265.3 97.2 %all-gather.22.cloned.1.call-done = bf16[1536,2560]{1,0:T(8,128)(2,1)} async-done(((bf16[1536,1280]{1,0:T(8,128)(2,1)}), bf16[1536,2560]{1,0:T(8,128)(2,1)}) %all-gather.22.cloned.1.call-update) | async-done | bytes 7864336 | tf_op jit(solution)/shard_map/all_gather | solution.py:309
  1362.5 5.7 fusion.32
  1369.7 3.5 all-to-all-start.1
  1374.3 5.5 all-to-all-done.1
  1379.8 3.6 all-to-all-start.4
  1383.5 51.0 %psum.7 = f32[2,1536]{1,0:T(2,128)S(1)} all-reduce(f32[2,1536]{1,0:T(2,128)S(1)} %pad_maximum_fusion.12), channel_id=1, replica_groups=mesh['dp'=4,'ctx'=4,'tensor'=2] {'dp','ctx','tensor'}, use_global_device_ids=true, to_apply=%region_20.21 | all-reduce | flops 3072 | bytes 24576 | tf_op jit(solution)/shard_map/psum | solution.py:322
  1435.2 82.5 %all-gather.26.cloned.1.call-done = bf16[4,4,384,1920]{3,2,1,0:T(8,128)(2,1)} async-done(((bf16[1,4,384,1920]{3,2,1,0:T(8,128)(2,1)}), bf16[4,4,384,1920]{3,2,1,0:T(8,128)(2,1)}) %all-gather.26.cloned.1.call-update) | async-done | bytes 23592976 | tf_op jit(solution)/shard_map/all_gather | solution.py:238
  1517.7 13.3 slice.177
  1531.0 21.0 %copy.313 = bf16[4,4,384,1280]{2,3,1,0:T(8,128)(2,1)} copy(bf16[4,4,384,1280]{3,2,1,0:T(8,128)(2,1)} %slice.177) | data formatting | bytes 31457280
  1552.0 57.4 %reduce-scatter.17.cloned.1.call-done = bf16[96,2088]{1,0:T(8,128)(2,1)} async-done(((bf16[1536,2088]{1,0:T(8,128)(2,1)}), bf16[96,2088]{1,0:T(8,128)(2,1)}) %reduce-scatter.17.cloned.1.call-update) | async-done | bytes 400912 | tf_op jit(solution)/shard_map/reduce_scatter | solution.py:319
  1609.4 9.2 convert_bitcast_fusion
  1618.6 10.5 copy.287
  1629.1 30.7 %copy.291 = f32[384,20,1024]{2,0,1:T(8,128)} copy(f32[384,20,1024]{0,2,1:T(8,128)} %bitcast.172) | data formatting | bytes 62914560
  1659.8 7.6 slice.178
  1667.4 10.6 copy.314
  1678.0 11.3 convert_bitcast_fusion.1
  1689.3 12.8 copy.289
  1702.1 15.7 copy.292
  (239 shorter events, 124.1 us)
Async XLA Ops:
  7.2 2.7 copy-start
  7.2 57.5 %all-gather.10.cloned.1.call-start = ((), (), s32[]{:S(2)}) async-start(), calls=%async_computation.9 | async-start | bytes 4595712 | tf_op jit(solution)/shard_map/all_gather | solution.py:104
  9.8 98.6 %all-gather.14.cloned.1.call-start = ((), (), s32[]{:S(2)}) async-start(), calls=%async_computation.11 | async-start | bytes 2506752 | tf_op jit(solution)/shard_map/all_gather | solution.py:106
  10.6 115.4 %all-gather.12.cloned.1.call-start = ((), (), s32[]{:S(2)}) async-start(), calls=%async_computation.10 | async-start | bytes 1310720 | tf_op jit(solution)/shard_map/all_gather | solution.py:168
  19.3 49.1 %copy-start.30 = (f32[1536]{0:T(1024)}, f32[1536]{0:T(1024)S(1)}, u32[]{:S(2)}) copy-start(f32[1536]{0:T(1024)S(1)} %get-tuple-element.95) | copy-start | bytes 18436
  30.9 163.4 %copy-start.5 = (bf16[256,1536]{0,1:T(8,128)(2,1)}, bf16[256,1536]{0,1:T(8,128)(2,1)S(1)}, u32[]{:S(2)}) copy-start(bf16[256,1536]{0,1:T(8,128)(2,1)S(1)} %all_gather.47) | copy-start | bytes 2359300
  31.1 37.6 %copy-start.36 = (f32[256]{0:T(256)}, f32[256]{0:T(256)S(1)}, u32[]{:S(2)}) copy-start(f32[256]{0:T(256)S(1)} %add_rsqrt_fusion) | copy-start | bytes 3076
  31.9 36.8 %copy-start.28 = (f32[256,32]{0,1:T(8,128)}, f32[256,32]{0,1:T(8,128)S(1)}, u32[]{:S(2)}) copy-start(f32[256,32]{0,1:T(8,128)S(1)} %get-tuple-element.131) | copy-start | bytes 98308
  68.2 1.8 copy-start.38
  68.2 40.4 %copy-start.35 = (s32[1,1024]{1,0:T(1,128)S(1)}, s32[1,1024]{1,0:T(1,128)}, u32[]{:S(2)}) copy-start(s32[1,1024]{1,0:T(1,128)} %param.15) | copy-start | bytes 12292
  69.7 124.5 %all-gather.16.cloned.1.call-start = ((), (), s32[]{:S(2)}) async-start(), calls=%async_computation.12 | async-start | bytes 7077888 | tf_op jit(solution)/shard_map/all_gather | solution.py:190
  108.9 22.6 %copy-start.20 = (bf16[256,12,64]{0,2,1:T(8,128)(2,1)}, bf16[256,12,64]{0,2,1:T(8,128)(2,1)S(1)}, u32[]{:S(2)}) copy-start(bf16[256,12,64]{0,2,1:T(8,128)(2,1)S(1)} %pad_maximum_fusion.9) | copy-start | bytes 1179652
  129.5 2.0 copy-start.18
  131.5 5.7 copy-start.2
  140.3 2.6 copy-start.3
  144.0 50.2 %copy-start.22 = (bf16[4,64,3,256]{3,1,2,0:T(8,128)(2,1)}, bf16[4,64,3,256]{3,1,2,0:T(8,128)(2,1)S(1)}, u32[]{:S(2)}) copy-start(bf16[4,64,3,256]{3,1,2,0:T(8,128)(2,1)S(1)} %convolution_convert_fusion.8) | copy-start | bytes 1179652
  144.9 56.1 %copy-start.27 = (bf16[256,768]{1,0:T(8,128)(2,1)S(1)}, bf16[256,768]{1,0:T(8,128)(2,1)}, u32[]{:S(2)}) copy-start(bf16[256,768]{1,0:T(8,128)(2,1)} %param.27) | copy-start | bytes 1179652
  144.9 49.3 %all-to-all-start = ((bf16[2,128,768]{1,2,0:T(8,128)(2,1)}), bf16[2,128,768]{1,2,0:T(8,128)(2,1)S(1)}, u32[]{:S(2)}, u32[]{:S(2)}) async-start(bf16[2,128,768]{1,2,0:T(8,128)(2,1)} %copy.259), calls=%async_computation | async-start | bytes 786432 | tf_op jit(solution)/shard_map/all_to_all | solution.py:189
  148.5 285.2 %all-gather.18.cloned.1.call-start = ((), (), s32[]{:S(2)}) async-start(), calls=%async_computation.13 | async-start | bytes 14057472 | tf_op jit(solution)/shard_map/all_gather | solution.py:200
  198.0 748.4 %copy-start.7 = (f32[128,1536]{0,1:T(8,128)}, f32[128,1536]{0,1:T(8,128)S(1)}, u32[]{:S(2)}) copy-start(f32[128,1536]{0,1:T(8,128)S(1)} %get-tuple-element.135) | copy-start | bytes 2359300
  201.0 359.6 %all-gather.20.cloned.1.call-start = ((), (), s32[]{:S(2)}) async-start(), calls=%async_computation.14 | async-start | bytes 12976128 | tf_op jit(solution)/shard_map/all_gather | solution.py:113
  211.1 731.6 %reduce-scatter.15.cloned.1.call-start = ((), (), s32[]{:S(2)}) async-start(), calls=%async_computation.20 | async-start | bytes 14057472
  242.5 49.2 %collective-permute-start = (bf16[1,384,1920]{1,2,0:T(8,128)(2,1)}, bf16[1,384,1920]{1,2,0:T(8,128)(2,1)}, u32[]{:S(2)}, u32[]{:S(2)}) collective-permute-start(bf16[1,384,1920]{1,2,0:T(8,128)(2,1)} %get-tuple-element.111), channel_id=1, source_target_pairs={{0,8},{8,16},{16,24},{24,0},{1,9},{9,17},{17,25},{25,1},{2,10},{10... | collective-permute-start | bytes 4423688 | tf_op jit(solution)/shard_map/ppermute | solution.py:61
  244.1 128.0 %collective-permute-start.1 = (bf16[1,384,1920]{1,2,0:T(8,128)(2,1)}, bf16[1,384,1920]{1,2,0:T(8,128)(2,1)}, u32[]{:S(2)}, u32[]{:S(2)}) collective-permute-start(bf16[1,384,1920]{1,2,0:T(8,128)(2,1)} %get-tuple-element.112), channel_id=1, source_target_pairs={{0,16},{8,24},{16,0},{24,8},{1,17},{9,25},{17,1},{25,9},{2,18},{10... | collective-permute-start | bytes 4423688 | tf_op jit(solution)/shard_map/ppermute | solution.py:61
  246.5 128.2 %collective-permute-start.2 = (bf16[1,384,1920]{1,2,0:T(8,128)(2,1)}, bf16[1,384,1920]{1,2,0:T(8,128)(2,1)}, u32[]{:S(2)}, u32[]{:S(2)}) collective-permute-start(bf16[1,384,1920]{1,2,0:T(8,128)(2,1)} %get-tuple-element.109), channel_id=1, source_target_pairs={{0,24},{8,0},{16,8},{24,16},{1,25},{9,1},{17,9},{25,17},{2,26},{10... | collective-permute-start | bytes 4423688 | tf_op jit(solution)/shard_map/ppermute | solution.py:61
  250.5 3.0 copy-start.14
  377.2 5.3 copy-start.15
  652.4 294.0 %copy-start.11 = (bf16[128,2,768]{0,2,1:T(8,128)(2,1)S(1)}, bf16[128,2,768]{0,2,1:T(8,128)(2,1)}, u32[]{:S(2)}) copy-start(bf16[128,2,768]{0,2,1:T(8,128)(2,1)} %copy.271) | copy-start | bytes 1179652
  652.4 557.6 %reduce-scatter.11.cloned.1.call-start = ((), (), s32[]{:S(2)}) async-start(), calls=%async_computation.15 | async-start | bytes 1310720 | tf_op jit(solution)/shard_map/reduce_scatter | solution.py:285
  944.0 17.7 %copy-start.24 = (bf16[1536,768]{1,0:T(8,128)(2,1)S(1)}, bf16[1536,768]{1,0:T(8,128)(2,1)}, u32[]{:S(2)}) copy-start(bf16[1536,768]{1,0:T(8,128)(2,1)} %all-gather.14.cloned.1.call-done) | copy-start | bytes 7077892
  963.4 12.7 slice-start
  969.1 7.0 slice-start.1
  969.1 7.2 slice-start.2
  976.3 4.8 copy-start.21
  981.1 4.9 copy-start.25
  987.1 277.0 %reduce-scatter.13.cloned.1.call-start = ((), (), s32[]{:S(2)}) async-start(), calls=%async_computation.19 | async-start | bytes 12976128
  990.9 2.4 copy-start.16
  1007.3 355.1 %all-gather.22.cloned.1.call-start = ((), (), s32[]{:S(2)}) async-start(), calls=%async_computation.16 | async-start | bytes 11796480 | tf_op jit(solution)/shard_map/all_gather | solution.py:309
  1011.7 505.9 %all-gather.26.cloned.1.call-start = ((), (), s32[]{:S(2)}) async-start(), calls=%async_computation.18 | async-start | bytes 29491200 | tf_op jit(solution)/shard_map/all_gather | solution.py:238
  1062.9 59.9 %collective-permute-start.3 = (bf16[1,384,1920]{2,1,0:T(8,128)(2,1)S(1)}, bf16[1,384,1920]{2,1,0:T(8,128)(2,1)S(1)}, u32[]{:S(2)}, u32[]{:S(2)}) collective-permute-start(bf16[1,384,1920]{2,1,0:T(8,128)(2,1)S(1)} %get-tuple-element.108), channel_id=1, source_target_pairs={{0,8},{8,16},{16,24},{24,0},{1,9},{9,17},{17,25},{25,1},{2,10},{10... | collective-permute-start | bytes 4423688 | tf_op jit(solution)/shard_map/ppermute | solution.py:61
  1064.0 132.0 %collective-permute-start.4 = (bf16[1,384,1920]{2,1,0:T(8,128)(2,1)S(1)}, bf16[1,384,1920]{2,1,0:T(8,128)(2,1)S(1)}, u32[]{:S(2)}, u32[]{:S(2)}) collective-permute-start(bf16[1,384,1920]{2,1,0:T(8,128)(2,1)S(1)} %get-tuple-element.107), channel_id=1, source_target_pairs={{0,16},{8,24},{16,0},{24,8},{1,17},{9,25},{17,1},{25,9},{2,18},{10... | collective-permute-start | bytes 4423688 | tf_op jit(solution)/shard_map/ppermute | solution.py:61
  1066.3 130.9 %collective-permute-start.5 = (bf16[1,384,1920]{2,1,0:T(8,128)(2,1)S(1)}, bf16[1,384,1920]{2,1,0:T(8,128)(2,1)S(1)}, u32[]{:S(2)}, u32[]{:S(2)}) collective-permute-start(bf16[1,384,1920]{2,1,0:T(8,128)(2,1)S(1)} %get-tuple-element.106), channel_id=1, source_target_pairs={{0,24},{8,0},{16,8},{24,16},{1,25},{9,1},{17,9},{25,17},{2,26},{10... | collective-permute-start | bytes 4423688 | tf_op jit(solution)/shard_map/ppermute | solution.py:61
  1198.5 410.9 %reduce-scatter.17.cloned.1.call-start = ((), (), s32[]{:S(2)}) async-start(), calls=%async_computation.21 | async-start | bytes 7102464 | tf_op jit(solution)/shard_map/reduce_scatter | solution.py:319
  1199.0 8.8 slice-start.3
  1199.0 5.6 slice-start.5
  1199.1 5.6 copy-start.13
  1199.1 6.6 copy-start.23
  1199.1 8.8 slice-start.4
  1204.6 3.2 copy-start.19
  1205.6 5.5 copy-start.29
  1205.6 5.5 copy-start.32
  1207.9 4.7 copy-start.31
  1207.9 4.7 copy-start.37
  1210.0 5.1 copy-start.4
  1210.0 5.1 copy-start.26
  1227.3 8.9 copy-start.6
  1232.7 129.8 %all-to-all-start.3 = ((bf16[2,128,1280]{1,2,0:T(8,128)(2,1)}), bf16[2,128,1280]{1,2,0:T(8,128)(2,1)S(1)}, u32[]{:S(2)}, u32[]{:S(2)}) async-start(bf16[2,128,1280]{1,2,0:T(8,128)(2,1)} %copy.277), calls=%async_computation.4 | async-start | bytes 1310720 | tf_op jit(solution)/shard_map/all_to_all | solution.py:310
  1362.5 5.7 copy-start.8
  1362.5 5.7 copy-start.10
  1368.2 15.3 copy-start.33
  1369.7 10.1 all-to-all-start.1
  1379.8 55.4 %all-to-all-start.4 = ((f32[128,2,768]{2,0,1:T(8,128)}), f32[128,2,768]{2,0,1:T(8,128)S(1)}, u32[]{:S(2)}, u32[]{:S(2)}) async-start(f32[128,2,768]{2,0,1:T(8,128)} %copy.279), calls=%async_computation.5 | async-start | bytes 1572864 | tf_op jit(solution)/shard_map/all_to_all | solution.py:316
  1383.4 334.4 %all-gather.24.cloned.1.call-start = ((), (), s32[]{:S(2)}) async-start(), calls=%async_computation.17 | async-start | bytes 2088960 | tf_op jit(solution)/shard_map/all_gather | solution.py:320
  1702.1 23.7 %copy-start.1 = (bf16[384,768]{1,0:T(8,128)(2,1)S(1)}, bf16[384,768]{1,0:T(8,128)(2,1)}, u32[]{:S(2)}) copy-start(bf16[384,768]{1,0:T(8,128)(2,1)} %param.22) | copy-start | bytes 1769476
  (4 other events, 4.2 us)
Sparse Core Ops, SparseCore 0:
  10.9 53.7 all-gather.9
  67.5 40.8 all-gather.13
  110.5 15.4 all-gather.11
  127.4 66.8 all-gather.15
  201.1 232.5 all-gather.17
  437.1 123.4 all-gather.19
  652.5 290.1 reduce-scatter.14
  987.2 23.9 reduce-scatter.10
  1017.8 246.2 reduce-scatter.12
  1265.5 96.9 all-gather.21
  1364.0 153.5 all-gather.25
  1521.5 87.8 reduce-scatter.16
  1611.0 19.1 all-gather.23
where the time goes:
time: 1750 us; the launch traced here: 1730 us
  waiting for transfers between devices  1080 us (62%)
  local copies, waits for them, and re-layouts  268 us (15%)
  matrix products  171 us (10%)
  blocking collectives  89.2 us (5%)
  other arithmetic  80.6 us (5%)
  starting transfers between devices  26 us (1%)
    unnamed x15, waiting for transfers between devices  318 us
    ppermute x6, waiting for transfers between devices, exchange(): lax.ppermute(sent, 'dp', [(i, (i + hop) % count) for i in range(count)])  236 us
    dot_general x16, matrix products, dot(): return lax.dot_general(a, b, (dims, ((), ())), preferred_element_type=F32)  148 us
    unnamed x103, local copies, waits for them, and re-layouts  133 us
    all_gather x1, waiting for transfers between devices, on_device(): cot_all = lax.all_gather(cot_sub, ALL, axis=0, tiled=True)  103 us
    all_gather x1, waiting for transfers between devices, on_device(): qkv_full = lax.all_gather(qkv_w, 'tensor', axis=1, tiled=True)  97.2 us
    all_gather x1, waiting for transfers between devices, on_device(): grad_expert = lax.all_gather(grad_expert, 'ctx', axis=0)  82.5 us
    reduce_scatter x1, waiting for transfers between devices, on_device(): lax.psum_scatter(weight_grads, ('dp', 'ctx'), scatter_dimension=0, tiled=...  57.4 us
  transfers between devices with their start and end apart: 23, of which 16 were waited for; matrix products, arithmetic and copies ran while one was open for 21% of the time, Pallas kernels for 0%

commit v1 on v0

--- a/solution.py
+++ b/solution.py
@@ -319,7 +319,7 @@
     weight_grads = lax.psum_scatter(weight_grads, ("dp", "ctx"), scatter_dimension=0, tiled=True)
     weight_grads = lax.all_gather(weight_grads, "ctx", axis=0, tiled=True).astype(F32)
     edges = [0, q_width, q_width + kv_width, qkv_width, qkv_width + q_width]
-    gain_grads = lax.psum(jnp.stack([grad_gain_one, grad_gain_two]), ALL)
+    gain_grads = jnp.sum(lax.all_gather(jnp.stack([grad_gain_one, grad_gain_two]), ALL), axis=0)
     gain_grads = lax.dynamic_slice_in_dim(gain_grads, tensor_at * part_width, part_width, 1)
     return (
         result,

time: 1750 us -> 1750 us (level)
  blocking collectives: 89.2 us -> 113 us
  waiting for transfers between devices: 1080 us -> 1060 us
    all_gather x0 -> x1, blocking collectives: none -> 75.1 us  [on_device(): lax.all_gather(jnp.stack([grad_gain_one, grad_gain_two]), ALL)]
    psum x1 -> x0, blocking collectives: 51 us -> none  [on_device(): gain_grads = lax.psum(jnp.stack([grad_gain_one, grad_gain_two]), ALL)]
    all_gather x1, waiting for transfers between devices: 82.5 us -> 59 us  [on_device(): grad_expert = lax.all_gather(grad_expert, 'ctx', axis=0)]
where the time goes in v1:
time: 1750 us; the launch traced here: 1730 us
  waiting for transfers between devices  1060 us (61%)
  local copies, waits for them, and re-layouts  268 us (15%)
  matrix products  171 us (10%)
  blocking collectives  113 us (6%)
  other arithmetic  80.7 us (5%)
  starting transfers between devices  26 us (1%)
    unnamed x15, waiting for transfers between devices  318 us
    ppermute x6, waiting for transfers between devices, exchange(): lax.ppermute(sent, 'dp', [(i, (i + hop) % count) for i in range(count)])  236 us
    dot_general x16, matrix products, dot(): return lax.dot_general(a, b, (dims, ((), ())), preferred_element_type=F32)  148 us
    unnamed x103, local copies, waits for them, and re-layouts  133 us
    all_gather x1, waiting for transfers between devices, on_device(): cot_all = lax.all_gather(cot_sub, ALL, axis=0, tiled=True)  103 us
    all_gather x1, waiting for transfers between devices, on_device(): qkv_full = lax.all_gather(qkv_w, 'tensor', axis=1, tiled=True)  97.2 us
    all_gather x1, blocking collectives, on_device(): lax.all_gather(jnp.stack([grad_gain_one, grad_gain_two]), ALL)  75.1 us
    all_gather x1, waiting for transfers between devices, on_device(): grad_expert = lax.all_gather(grad_expert, 'ctx', axis=0)  59 us
  transfers between devices with their start and end apart: 23, of which 16 were waited for; matrix products, arithmetic and copies ran while one was open for 21% of the time, Pallas kernels for 0%

profile of v1, /device:TPU:0, one launch (start us, length us, event | category | flops | bytes accessed | tf_op | source)
XLA Modules:
  0.0 1733.2 jit_solution(16816478552106769148)
XLA Ops:
  13.2 5.3 all_gather.54
  20.2 10.7 all_gather.53
  31.9 32.8 %all-gather.12.cloned.1.call-done = bf16[1536,1320]{1,0:T(8,128)(2,1)} async-done(((bf16[96,1320]{1,0:T(8,128)(2,1)}), bf16[1536,1320]{1,0:T(8,128)(2,1)}) %all-gather.12.cloned.1.call-update) | async-done | bytes 4055056 | tf_op jit(solution)/shard_map/all_gather | solution.py:104
  64.7 3.4 fusion.51
  70.5 37.9 %all-gather.16.cloned.1.call-done = bf16[1536,768]{1,0:T(8,128)(2,1)} async-done(((bf16[96,768]{1,0:T(8,128)(2,1)}), bf16[1536,768]{1,0:T(8,128)(2,1)}) %all-gather.16.cloned.1.call-update) | async-done | bytes 2359312 | tf_op jit(solution)/shard_map/all_gather | solution.py:106
  108.9 17.1 all-gather.14.cloned.1.call-done
  134.1 3.2 copy-done.2
  144.9 3.6 all-to-all-start
  149.1 45.2 %all-gather.18.cloned.1.call-done = bf16[1536,1536]{1,0:T(8,128)(2,1)} async-done(((bf16[1536,768]{1,0:T(8,128)(2,1)}), bf16[1536,1536]{1,0:T(8,128)(2,1)}) %all-gather.18.cloned.1.call-update) | async-done | bytes 4718608 | tf_op jit(solution)/shard_map/all_gather | solution.py:190
  194.3 3.7 multiply_reduce_fusion.2
  201.1 9.1 all_to_all.92
  211.2 4.7 constant_dynamic-slice_fusion.4
  215.9 6.3 copy.311
  222.2 4.7 copy.262
  230.0 4.0 copy.312
  234.0 3.1 copy.264
  237.1 5.4 fusion.17
  254.7 37.0 %collective-permute-done = bf16[1,384,1920]{1,2,0:T(8,128)(2,1)} collective-permute-done((bf16[1,384,1920]{1,2,0:T(8,128)(2,1)}, bf16[1,384,1920]{1,2,0:T(8,128)(2,1)}, u32[]{:S(2)}, u32[]{:S(2)}) %collective-permute-start) | collective-permute-done | bytes 1474592 | tf_op jit(solution)/shard_map/ppermute | solution.py:61
  294.3 77.8 %collective-permute-done.1 = bf16[1,384,1920]{1,2,0:T(8,128)(2,1)} collective-permute-done((bf16[1,384,1920]{1,2,0:T(8,128)(2,1)}, bf16[1,384,1920]{1,2,0:T(8,128)(2,1)}, u32[]{:S(2)}, u32[]{:S(2)}) %collective-permute-start.1) | collective-permute-done | bytes 1474592 | tf_op jit(solution)/shard_map/ppermute | solution.py:61
  383.8 50.0 %all-gather.20.cloned.1.call-done = bf16[4096,1664]{0,1:T(8,128)(2,1)} async-done(((bf16[128,1664]{0,1:T(8,128)(2,1)}), bf16[4096,1664]{0,1:T(8,128)(2,1)}) %all-gather.20.cloned.1.call-update) | async-done | bytes 13631504 | tf_op jit(solution)/shard_map/all_gather | solution.py:200
  434.9 22.6 %fusion.8 = f32[4096,1280]{0,1:T(8,128)} fusion(bf16[1536,1920]{1,0:T(8,128)(2,1)} %bitcast.22, bf16[4096,1664]{0,1:T(8,128)(2,1)} %all-gather.20.cloned.1.call-done), kind=kOutput, calls=%fused_computation.41 | convolution fusion | flops 16106127360 | bytes 37486592 | tf_op jit(solution)/shard_map/dot_general | solution.py:40
  457.6 103.0 %all-gather.22.cloned.1.call-done = bf16[4096,1536]{0,1:T(8,128)(2,1)} async-done(((bf16[128,1536]{0,1:T(8,128)(2,1)}), bf16[4096,1536]{0,1:T(8,128)(2,1)}) %all-gather.22.cloned.1.call-update) | async-done | bytes 12582928 | tf_op jit(solution)/shard_map/all_gather | solution.py:113
  560.6 28.3 %multiply_convert_fusion.1 = (bf16[4096,640]{0,1:T(8,128)(2,1)}, bf16[4096,640]{0,1:T(8,128)(2,1)}, f32[4096,640]{0,1:T(8,128)}, bf16[4096,640]{0,1:T(8,128)(2,1)}) fusion(f32[4096,1280]{0,1:T(8,128)} %fusion.8, f32[4096,5]{0,1:T(8,128)S(1)} %convert_add_fusion.1, bf16[4096,1536]{0,1:T(8,128)(2,1)} %all-gather.22.cloned.1.call-done, ...), kind=kOutput, calls=%fused_computation.21 | convolution fusion | flops 8100249600 | bytes 61816832 | tf_op jit(solution)/shard_map/dot_general | solution.py:40
  588.9 4.7 reduce_sum.141
  593.6 23.4 %convolution_convert_fusion.1 = bf16[4096,1536]{0,1:T(8,128)(2,1)} fusion(bf16[4096,640]{0,1:T(8,128)(2,1)} %get-tuple-element.101, bf16[4096,640]{0,1:T(8,128)(2,1)} %get-tuple-element.100, bf16[1536,1920]{1,0:T(8,128)(2,1)} %bitcast.22), kind=kOutput, calls=%fused_computation.5 | convolution fusion | flops 16133390336 | bytes 27000832 | tf_op jit(solution)/shard_map/dot_general | solution.py:40
  619.7 14.8 pad_maximum_fusion
  634.4 17.9 %copy.306 = bf16[4096,1664]{1,0:T(8,128)(2,1)} copy(bf16[4096,1664]{0,1:T(8,128)(2,1)} %pad_maximum_fusion) | data formatting | bytes 27262976
  652.5 290.2 %reduce-scatter.15.cloned.1.call-done = bf16[128,1664]{1,0:T(8,128)(2,1)} async-done(((bf16[4096,1664]{1,0:T(8,128)(2,1)}), bf16[128,1664]{1,0:T(8,128)(2,1)}) %reduce-scatter.15.cloned.1.call-update) | async-done | bytes 426000
  947.6 13.2 all_gather.61
  963.4 5.7 fusion.24
  969.1 6.9 fusion
  976.3 4.8 fusion.2
  981.1 4.8 fusion.23
  987.1 3.8 fusion.4
  993.3 14.0 convolution_convert_fusion
  1007.4 4.3 slice.148
  1011.8 13.1 fusion.10
  1024.9 23.4 %convolution_convert_fusion.2 = bf16[1536,1280]{0,1:T(8,128)(2,1)S(1)} fusion(bf16[4096,640]{0,1:T(8,128)(2,1)} %get-tuple-element.101, bf16[4096,640]{0,1:T(8,128)(2,1)} %get-tuple-element.100, bf16[4096,1664]{0,1:T(8,128)(2,1)} %all-gather.20.cloned.1.call-done), kind=kOutput, calls=%fused_computation.29 | convolution fusion | flops 16129064960 | bytes 27000832 | tf_op jit(solution)/shard_map/dot_general | solution.py:40
  1051.3 8.8 copy.310
  1073.4 49.4 %collective-permute-done.3 = bf16[1,384,1920]{2,1,0:T(8,128)(2,1)S(1)} collective-permute-done((bf16[1,384,1920]{2,1,0:T(8,128)(2,1)S(1)}, bf16[1,384,1920]{2,1,0:T(8,128)(2,1)S(1)}, u32[]{:S(2)}, u32[]{:S(2)}) %collective-permute-start.3) | collective-permute-done | bytes 1474592 | tf_op jit(solution)/shard_map/ppermute | solution.py:61
  1124.1 72.0 %collective-permute-done.4 = bf16[1,384,1920]{2,1,0:T(8,128)(2,1)S(1)} collective-permute-done((bf16[1,384,1920]{2,1,0:T(8,128)(2,1)S(1)}, bf16[1,384,1920]{2,1,0:T(8,128)(2,1)S(1)}, u32[]{:S(2)}, u32[]{:S(2)}) %collective-permute-start.4) | collective-permute-done | bytes 1474592 | tf_op jit(solution)/shard_map/ppermute | solution.py:61
  1199.1 5.5 slice-done.5
  1218.1 9.2 copy.308
  1227.5 4.2 pad_maximum_fusion.7
  1232.7 3.5 all-to-all-start.3
  1236.4 27.6 %reduce-scatter.13.cloned.1.call-done = bf16[128,1536]{1,0:T(8,128)(2,1)} async-done(((bf16[4096,1536]{1,0:T(8,128)(2,1)}), bf16[128,1536]{1,0:T(8,128)(2,1)}) %reduce-scatter.13.cloned.1.call-update) | async-done | bytes 393232
  1265.3 97.2 %all-gather.24.cloned.1.call-done = bf16[1536,2560]{1,0:T(8,128)(2,1)} async-done(((bf16[1536,1280]{1,0:T(8,128)(2,1)}), bf16[1536,2560]{1,0:T(8,128)(2,1)}) %all-gather.24.cloned.1.call-update) | async-done | bytes 7864336 | tf_op jit(solution)/shard_map/all_gather | solution.py:309
  1362.5 5.7 fusion.32
  1369.7 3.5 all-to-all-start.1
  1374.3 5.5 all-to-all-done.1
  1379.8 3.6 all-to-all-start.4
  1383.5 75.1 %all-gather.1 = f32[32,2,1536]{2,1,0:T(2,128)S(1)} all-gather(f32[1,2,1536]{2,1,0:T(2,128)S(1)} %maximum_bitcast_fusion), channel_id=2, replica_groups=mesh['dp'=4,'ctx'=4,'tensor'=2] {'dp','ctx','tensor'}, dimensions={0}, use_global_device_ids=true | all-gather | bytes 405504 | tf_op jit(solution)/shard_map/all_gather | solution.py:322
  1459.4 59.0 %all-gather.28.cloned.1.call-done = bf16[4,4,384,1920]{3,2,1,0:T(8,128)(2,1)} async-done(((bf16[1,4,384,1920]{3,2,1,0:T(8,128)(2,1)}), bf16[4,4,384,1920]{3,2,1,0:T(8,128)(2,1)}) %all-gather.28.cloned.1.call-update) | async-done | bytes 23592976 | tf_op jit(solution)/shard_map/all_gather | solution.py:238
  1518.4 13.3 slice.177
  1531.7 21.0 %copy.313 = bf16[4,4,384,1280]{2,3,1,0:T(8,128)(2,1)} copy(bf16[4,4,384,1280]{3,2,1,0:T(8,128)(2,1)} %slice.177) | data formatting | bytes 31457280
  1552.7 57.3 %reduce-scatter.17.cloned.1.call-done = bf16[96,2088]{1,0:T(8,128)(2,1)} async-done(((bf16[1536,2088]{1,0:T(8,128)(2,1)}), bf16[96,2088]{1,0:T(8,128)(2,1)}) %reduce-scatter.17.cloned.1.call-update) | async-done | bytes 400912 | tf_op jit(solution)/shard_map/reduce_scatter | solution.py:319
  1610.0 9.2 convert_bitcast_fusion
  1619.2 10.5 copy.287
  1629.7 30.7 %copy.291 = f32[384,20,1024]{2,0,1:T(8,128)} copy(f32[384,20,1024]{0,2,1:T(8,128)} %bitcast.174) | data formatting | bytes 62914560
  1660.4 7.6 slice.178
  1668.0 10.6 copy.314
  1678.6 11.3 convert_bitcast_fusion.1
  1689.9 12.8 copy.289
  1702.7 15.7 copy.292
  (240 shorter events, 124.2 us)
Async XLA Ops:
  7.2 2.7 copy-start
  7.2 57.5 %all-gather.12.cloned.1.call-start = ((), (), s32[]{:S(2)}) async-start(), calls=%async_computation.9 | async-start | bytes 4595712 | tf_op jit(solution)/shard_map/all_gather | solution.py:104
  9.8 98.6 %all-gather.16.cloned.1.call-start = ((), (), s32[]{:S(2)}) async-start(), calls=%async_computation.11 | async-start | bytes 2506752 | tf_op jit(solution)/shard_map/all_gather | solution.py:106
  10.6 115.4 %all-gather.14.cloned.1.call-start = ((), (), s32[]{:S(2)}) async-start(), calls=%async_computation.10 | async-start | bytes 1310720 | tf_op jit(solution)/shard_map/all_gather | solution.py:168
  19.3 49.1 %copy-start.30 = (f32[1536]{0:T(1024)}, f32[1536]{0:T(1024)S(1)}, u32[]{:S(2)}) copy-start(f32[1536]{0:T(1024)S(1)} %get-tuple-element.95) | copy-start | bytes 18436
  30.9 163.4 %copy-start.5 = (bf16[256,1536]{0,1:T(8,128)(2,1)}, bf16[256,1536]{0,1:T(8,128)(2,1)S(1)}, u32[]{:S(2)}) copy-start(bf16[256,1536]{0,1:T(8,128)(2,1)S(1)} %all_gather.53) | copy-start | bytes 2359300
  31.1 37.6 %copy-start.36 = (f32[256]{0:T(256)}, f32[256]{0:T(256)S(1)}, u32[]{:S(2)}) copy-start(f32[256]{0:T(256)S(1)} %add_rsqrt_fusion) | copy-start | bytes 3076
  31.9 36.8 %copy-start.28 = (f32[256,32]{0,1:T(8,128)}, f32[256,32]{0,1:T(8,128)S(1)}, u32[]{:S(2)}) copy-start(f32[256,32]{0,1:T(8,128)S(1)} %get-tuple-element.131) | copy-start | bytes 98308
  68.2 1.8 copy-start.38
  68.2 40.4 %copy-start.35 = (s32[1,1024]{1,0:T(1,128)S(1)}, s32[1,1024]{1,0:T(1,128)}, u32[]{:S(2)}) copy-start(s32[1,1024]{1,0:T(1,128)} %param.15) | copy-start | bytes 12292
  69.7 124.5 %all-gather.18.cloned.1.call-start = ((), (), s32[]{:S(2)}) async-start(), calls=%async_computation.12 | async-start | bytes 7077888 | tf_op jit(solution)/shard_map/all_gather | solution.py:190
  108.9 22.6 %copy-start.20 = (bf16[256,12,64]{0,2,1:T(8,128)(2,1)}, bf16[256,12,64]{0,2,1:T(8,128)(2,1)S(1)}, u32[]{:S(2)}) copy-start(bf16[256,12,64]{0,2,1:T(8,128)(2,1)S(1)} %pad_maximum_fusion.9) | copy-start | bytes 1179652
  129.5 2.0 copy-start.18
  131.5 5.7 copy-start.2
  140.3 2.6 copy-start.3
  144.0 50.2 %copy-start.22 = (bf16[4,64,3,256]{3,1,2,0:T(8,128)(2,1)}, bf16[4,64,3,256]{3,1,2,0:T(8,128)(2,1)S(1)}, u32[]{:S(2)}) copy-start(bf16[4,64,3,256]{3,1,2,0:T(8,128)(2,1)S(1)} %convolution_convert_fusion.8) | copy-start | bytes 1179652
  144.9 56.1 %copy-start.27 = (bf16[256,768]{1,0:T(8,128)(2,1)S(1)}, bf16[256,768]{1,0:T(8,128)(2,1)}, u32[]{:S(2)}) copy-start(bf16[256,768]{1,0:T(8,128)(2,1)} %param.27) | copy-start | bytes 1179652
  144.9 49.3 %all-to-all-start = ((bf16[2,128,768]{1,2,0:T(8,128)(2,1)}), bf16[2,128,768]{1,2,0:T(8,128)(2,1)S(1)}, u32[]{:S(2)}, u32[]{:S(2)}) async-start(bf16[2,128,768]{1,2,0:T(8,128)(2,1)} %copy.259), calls=%async_computation | async-start | bytes 786432 | tf_op jit(solution)/shard_map/all_to_all | solution.py:189
  148.5 285.2 %all-gather.20.cloned.1.call-start = ((), (), s32[]{:S(2)}) async-start(), calls=%async_computation.13 | async-start | bytes 14057472 | tf_op jit(solution)/shard_map/all_gather | solution.py:200
  198.0 748.4 %copy-start.7 = (f32[128,1536]{0,1:T(8,128)}, f32[128,1536]{0,1:T(8,128)S(1)}, u32[]{:S(2)}) copy-start(f32[128,1536]{0,1:T(8,128)S(1)} %get-tuple-element.135) | copy-start | bytes 2359300
  201.0 359.6 %all-gather.22.cloned.1.call-start = ((), (), s32[]{:S(2)}) async-start(), calls=%async_computation.14 | async-start | bytes 12976128 | tf_op jit(solution)/shard_map/all_gather | solution.py:113
  211.1 731.6 %reduce-scatter.15.cloned.1.call-start = ((), (), s32[]{:S(2)}) async-start(), calls=%async_computation.20 | async-start | bytes 14057472
  242.5 49.2 %collective-permute-start = (bf16[1,384,1920]{1,2,0:T(8,128)(2,1)}, bf16[1,384,1920]{1,2,0:T(8,128)(2,1)}, u32[]{:S(2)}, u32[]{:S(2)}) collective-permute-start(bf16[1,384,1920]{1,2,0:T(8,128)(2,1)} %get-tuple-element.111), channel_id=1, source_target_pairs={{0,8},{8,16},{16,24},{24,0},{1,9},{9,17},{17,25},{25,1},{2,10},{10... | collective-permute-start | bytes 4423688 | tf_op jit(solution)/shard_map/ppermute | solution.py:61
  244.1 128.0 %collective-permute-start.1 = (bf16[1,384,1920]{1,2,0:T(8,128)(2,1)}, bf16[1,384,1920]{1,2,0:T(8,128)(2,1)}, u32[]{:S(2)}, u32[]{:S(2)}) collective-permute-start(bf16[1,384,1920]{1,2,0:T(8,128)(2,1)} %get-tuple-element.112), channel_id=1, source_target_pairs={{0,16},{8,24},{16,0},{24,8},{1,17},{9,25},{17,1},{25,9},{2,18},{10... | collective-permute-start | bytes 4423688 | tf_op jit(solution)/shard_map/ppermute | solution.py:61
  246.5 128.2 %collective-permute-start.2 = (bf16[1,384,1920]{1,2,0:T(8,128)(2,1)}, bf16[1,384,1920]{1,2,0:T(8,128)(2,1)}, u32[]{:S(2)}, u32[]{:S(2)}) collective-permute-start(bf16[1,384,1920]{1,2,0:T(8,128)(2,1)} %get-tuple-element.109), channel_id=1, source_target_pairs={{0,24},{8,0},{16,8},{24,16},{1,25},{9,1},{17,9},{25,17},{2,26},{10... | collective-permute-start | bytes 4423688 | tf_op jit(solution)/shard_map/ppermute | solution.py:61
  250.5 3.0 copy-start.14
  377.2 5.3 copy-start.15
  652.4 294.0 %copy-start.11 = (bf16[128,2,768]{0,2,1:T(8,128)(2,1)S(1)}, bf16[128,2,768]{0,2,1:T(8,128)(2,1)}, u32[]{:S(2)}) copy-start(bf16[128,2,768]{0,2,1:T(8,128)(2,1)} %copy.271) | copy-start | bytes 1179652
  652.4 557.6 %reduce-scatter.11.cloned.1.call-start = ((), (), s32[]{:S(2)}) async-start(), calls=%async_computation.15 | async-start | bytes 1310720 | tf_op jit(solution)/shard_map/reduce_scatter | solution.py:285
  944.0 17.7 %copy-start.24 = (bf16[1536,768]{1,0:T(8,128)(2,1)S(1)}, bf16[1536,768]{1,0:T(8,128)(2,1)}, u32[]{:S(2)}) copy-start(bf16[1536,768]{1,0:T(8,128)(2,1)} %all-gather.16.cloned.1.call-done) | copy-start | bytes 7077892
  963.4 12.7 slice-start
  969.1 7.0 slice-start.1
  969.1 7.2 slice-start.2
  976.3 4.8 copy-start.21
  981.1 4.9 copy-start.25
  987.1 277.0 %reduce-scatter.13.cloned.1.call-start = ((), (), s32[]{:S(2)}) async-start(), calls=%async_computation.19 | async-start | bytes 12976128
  990.9 2.4 copy-start.16
  1007.3 355.1 %all-gather.24.cloned.1.call-start = ((), (), s32[]{:S(2)}) async-start(), calls=%async_computation.16 | async-start | bytes 11796480 | tf_op jit(solution)/shard_map/all_gather | solution.py:309
  1011.7 506.6 %all-gather.28.cloned.1.call-start = ((), (), s32[]{:S(2)}) async-start(), calls=%async_computation.18 | async-start | bytes 29491200 | tf_op jit(solution)/shard_map/all_gather | solution.py:238
  1062.9 59.9 %collective-permute-start.3 = (bf16[1,384,1920]{2,1,0:T(8,128)(2,1)S(1)}, bf16[1,384,1920]{2,1,0:T(8,128)(2,1)S(1)}, u32[]{:S(2)}, u32[]{:S(2)}) collective-permute-start(bf16[1,384,1920]{2,1,0:T(8,128)(2,1)S(1)} %get-tuple-element.108), channel_id=1, source_target_pairs={{0,8},{8,16},{16,24},{24,0},{1,9},{9,17},{17,25},{25,1},{2,10},{10... | collective-permute-start | bytes 4423688 | tf_op jit(solution)/shard_map/ppermute | solution.py:61
  1064.0 132.0 %collective-permute-start.4 = (bf16[1,384,1920]{2,1,0:T(8,128)(2,1)S(1)}, bf16[1,384,1920]{2,1,0:T(8,128)(2,1)S(1)}, u32[]{:S(2)}, u32[]{:S(2)}) collective-permute-start(bf16[1,384,1920]{2,1,0:T(8,128)(2,1)S(1)} %get-tuple-element.107), channel_id=1, source_target_pairs={{0,16},{8,24},{16,0},{24,8},{1,17},{9,25},{17,1},{25,9},{2,18},{10... | collective-permute-start | bytes 4423688 | tf_op jit(solution)/shard_map/ppermute | solution.py:61
  1066.3 130.9 %collective-permute-start.5 = (bf16[1,384,1920]{2,1,0:T(8,128)(2,1)S(1)}, bf16[1,384,1920]{2,1,0:T(8,128)(2,1)S(1)}, u32[]{:S(2)}, u32[]{:S(2)}) collective-permute-start(bf16[1,384,1920]{2,1,0:T(8,128)(2,1)S(1)} %get-tuple-element.106), channel_id=1, source_target_pairs={{0,24},{8,0},{16,8},{24,16},{1,25},{9,1},{17,9},{25,17},{2,26},{10... | collective-permute-start | bytes 4423688 | tf_op jit(solution)/shard_map/ppermute | solution.py:61
  1198.5 411.5 %reduce-scatter.17.cloned.1.call-start = ((), (), s32[]{:S(2)}) async-start(), calls=%async_computation.21 | async-start | bytes 7102464 | tf_op jit(solution)/shard_map/reduce_scatter | solution.py:319
  1199.0 8.8 slice-start.3
  1199.0 5.6 slice-start.5
  1199.1 5.6 copy-start.13
  1199.1 6.6 copy-start.23
  1199.1 8.8 slice-start.4
  1204.6 3.2 copy-start.19
  1205.6 5.5 copy-start.29
  1205.6 5.5 copy-start.32
  1207.9 4.7 copy-start.31
  1207.9 4.7 copy-start.37
  1210.0 5.1 copy-start.4
  1210.0 5.1 copy-start.26
  1227.3 8.9 copy-start.6
  1232.7 129.8 %all-to-all-start.3 = ((bf16[2,128,1280]{1,2,0:T(8,128)(2,1)}), bf16[2,128,1280]{1,2,0:T(8,128)(2,1)S(1)}, u32[]{:S(2)}, u32[]{:S(2)}) async-start(bf16[2,128,1280]{1,2,0:T(8,128)(2,1)} %copy.277), calls=%async_computation.4 | async-start | bytes 1310720 | tf_op jit(solution)/shard_map/all_to_all | solution.py:310
  1362.5 5.7 copy-start.8
  1362.5 5.7 copy-start.10
  1368.2 5.0 copy-start.33
  1369.7 10.1 all-to-all-start.1
  1379.8 79.6 %all-to-all-start.4 = ((f32[128,2,768]{2,0,1:T(8,128)}), f32[128,2,768]{2,0,1:T(8,128)S(1)}, u32[]{:S(2)}, u32[]{:S(2)}) async-start(f32[128,2,768]{2,0,1:T(8,128)} %copy.279), calls=%async_computation.5 | async-start | bytes 1572864 | tf_op jit(solution)/shard_map/all_to_all | solution.py:316
  1383.4 335.0 %all-gather.26.cloned.1.call-start = ((), (), s32[]{:S(2)}) async-start(), calls=%async_computation.17 | async-start | bytes 2088960 | tf_op jit(solution)/shard_map/all_gather | solution.py:320
  1702.7 23.7 %copy-start.1 = (bf16[384,768]{1,0:T(8,128)(2,1)S(1)}, bf16[384,768]{1,0:T(8,128)(2,1)}, u32[]{:S(2)}) copy-start(bf16[384,768]{1,0:T(8,128)(2,1)} %param.22) | copy-start | bytes 1769476
  (4 other events, 4.2 us)
Sparse Core Ops, SparseCore 0:
  10.9 53.7 all-gather.11
  67.5 40.8 all-gather.15
  110.5 15.4 all-gather.13
  127.4 66.8 all-gather.17
  201.1 232.5 all-gather.19
  437.1 123.4 all-gather.21
  652.5 290.1 reduce-scatter.14
  987.2 23.9 reduce-scatter.10
  1017.8 246.2 reduce-scatter.12
  1265.5 96.9 all-gather.23
  1364.0 154.2 all-gather.27
  1522.2 87.6 reduce-scatter.16
  1611.5 19.4 all-gather.25
